TPU v7x, 32 devices: a whole 2x2x4 slice. The times are simulated.
32 devices in a mesh: ctx: 16 (over z, x, core), head: 2 (over y).
Axes of the slice: x: 2, y: 2, z: 4, core: 2. Of those that a mesh axis runs over, the one named last changes fastest.
Arguments:
- inputs: bfloat16 [2048, 4096], P('ctx', 'head'), may hold values from -60 to 60
- out_grad: bfloat16 [2048, 4096], P('ctx', 'head'), may hold values from -6 to 6
- norm_gain: float32 [4096], replicated, may hold values from 0.5 to 1.5
- w_query: bfloat16 [4096, 4096], P(None, 'head'), may hold values from -2 to 2
- w_key: bfloat16 [4096, 1024], P(None, 'head'), may hold values from -2 to 2
- w_value: bfloat16 [4096, 1024], P(None, 'head'), may hold values from -0.09375 to 0.09375
- w_out: bfloat16 [4096, 4096], P('head'), may hold values from -0.09375 to 0.09375
- record_lengths: int32 [8], replicated, may hold values from 1 to 1024, 2048 in all
- block_order: int32 [32], replicated, may hold values from 0 to 31, each once
Outputs:
- input_grad: bfloat16 [2048, 4096], P('ctx', 'head')
- saliency: float32 [2048], P('ctx')
Inputs may be any that keep to these rules, and one draw needn't show every extreme that they name: `record_lengths`: record lengths sum to 2048. `block_order`: each number once.
All inputs are finite; a program needn't handle non-finite values.
Results may differ from a plain program's by a relative error of at most 0.007.
Values may be sent and summed in bfloat16 or wider, within the bound.
A program may use at most 128 MiB of HBM per device.

v0:
```python
import functools

import jax
import jax.numpy as jnp
from jax import lax
from jax.experimental import pallas as pl
from jax.experimental.pallas import tpu as pltpu
from jax.sharding import PartitionSpec as P

HEAD_DIM = 128
BLOCK = 64
NT = (((1,), (1,)), ((), ()))
TN = (((0,), (0,)), ((), ()))
F32 = jnp.float32
BF16 = jnp.bfloat16
MESH = pl.DeviceIdType.MESH
VM = pl.BlockSpec(memory_space=pltpu.VMEM)
ANY = pl.BlockSpec(memory_space=pl.ANY)
SM = pl.BlockSpec(memory_space=pltpu.SMEM)
VMEM_LIMIT = 64 * 1024 * 1024 - 128 * 1024


def timeline_place(stored, order_ref, lengths_ref):
    block = jnp.right_shift(stored, 6)
    position = jnp.zeros(stored.shape, jnp.int32)
    for b in range(order_ref.shape[0]):
        position = jnp.where(block == b, order_ref[b], position)
    position = position * BLOCK + (stored & (BLOCK - 1))
    record = jnp.zeros(stored.shape, jnp.int32)
    start = 0
    for r in range(lengths_ref.shape[0]):
        record = record + jnp.where(position >= start, 1, 0)
        start = start + lengths_ref[r]
    return position, record


def coords():
    me = lax.axis_index("ctx")
    return me, me // 4, lax.rem(me // 2, 2), lax.rem(me, 2)


def slot_of(z, x, c):
    return (z * 2 + x) * 2 + c


def enter(nz, nh):
    _, z, x, c = coords()
    head = lax.axis_index("head")
    barrier = pltpu.get_barrier_semaphore()

    def greet(target):
        pl.semaphore_signal(barrier, inc=1, device_id=target, device_id_type=MESH)

    for p in range(1, nh):
        greet({"head": lax.rem(head + p, nh)})
    greet({"ctx": slot_of(z, 1 - x, c)})
    greet({"ctx": slot_of(z, x, 1 - c)})

    @pl.when(z > 0)
    def _():
        greet({"ctx": slot_of(z - 1, x, c)})

    @pl.when(z < nz - 1)
    def _():
        greet({"ctx": slot_of(z + 1, x, c)})

    @pl.when((z > 0) & (z < nz - 1))
    def _():
        pl.semaphore_wait(barrier, nh + 3)

    @pl.when((z == 0) | (z == nz - 1))
    def _():
        pl.semaphore_wait(barrier, nh + 2)


def front_kernel(nz, nh, order_ref, lengths_ref, x_ref, dy_ref, gain_ref,
                 wq_ref, wk_ref, wv_ref, wo_ref,
                 q_out, do_out, kv_out, stat_ref, pq_ref, pk_ref,
                 q_ref, do_ref, kv_ref, wq, wk, wv, wo, xall, dyall, normed,
                 wsem, lsem, osem, ssem, xs, xr, dys, dyr, ks, kr):
    me, z, x, c = coords()
    head = lax.axis_index("head")
    rows, share = x_ref.shape
    dim = nh * share
    hq = q_ref.shape[1]
    width = wk_ref.shape[1]
    loads = [
        pltpu.make_async_copy(a, b, wsem.at[i])
        for i, (a, b) in enumerate(((wk_ref, wk), (wv_ref, wv), (wq_ref, wq), (wo_ref, wo)))
    ]
    for load in loads:
        load.start()
    own = [
        pltpu.make_async_copy(x_ref, xall.at[head], lsem.at[0]),
        pltpu.make_async_copy(dy_ref, dyall.at[head], lsem.at[1]),
    ]
    for copy in own:
        copy.start()
    enter(nz, nh)

    def head_copies(src, dst, send, recv):
        return [
            pltpu.make_async_remote_copy(
                src_ref=src, dst_ref=dst.at[head], send_sem=send.at[p - 1], recv_sem=recv.at[p - 1],
                device_id={"head": lax.rem(head + p, nh)}, device_id_type=MESH)
            for p in range(1, nh)
        ]

    xc = head_copies(x_ref, xall, xs, xr)
    dyc = head_copies(dy_ref, dyall, dys, dyr)
    for copy in xc + dyc:
        copy.start()
    length = kv_ref.shape[0]
    pk_ref[0:1, :], pk_ref[1:2, :] = timeline_place(
        lax.broadcasted_iota(jnp.int32, (1, length), 1), order_ref, lengths_ref)
    pq_ref[:, 0:1], pq_ref[:, 1:2] = timeline_place(
        lax.broadcasted_iota(jnp.int32, (rows, 1), 0) + me * rows, order_ref, lengths_ref)
    own[0].wait()
    for copy in xc:
        copy.wait()
    total = jnp.zeros((rows, 1), F32)
    for j in range(nh):
        v = xall[j].astype(F32)
        total = total + jnp.sum(v * v, axis=1, keepdims=True)
    root = jnp.sqrt(total / dim + 1e-05)
    inv = 1.0 / root
    for j in range(nh):
        cols = slice(j * share, (j + 1) * share)
        normed[:, cols] = (xall[j].astype(F32) * inv * gain_ref[:, cols]).astype(BF16)

    def block(slot):
        return kv_ref.at[pl.ds(pl.multiple_of(slot * rows, rows), rows), :]

    def send(direction, slot, target):
        return pltpu.make_async_remote_copy(
            src_ref=block(slot), dst_ref=block(slot), send_sem=ks.at[direction, slot],
            recv_sem=kr.at[slot], device_id={"ctx": target}, device_id_type=MESH)

    def store(slot):
        return pltpu.make_async_copy(
            block(slot), kv_out.at[pl.ds(pl.multiple_of(slot * rows, rows), rows), :],
            ssem.at[slot])

    def arrived(slot):
        send(0, slot, me).wait_recv()
        store(slot).start()

    mine = pl.ds(pl.multiple_of(me * rows, rows), rows)
    loads[0].wait()
    kv_ref[mine, :width] = jnp.dot(normed[...], wk[...], preferred_element_type=F32).astype(BF16)
    loads[1].wait()
    kv_ref[mine, width:] = jnp.dot(normed[...], wv[...], preferred_element_type=F32).astype(BF16)

    right = slot_of(z + 1, x, c)
    left = slot_of(z - 1, x, c)
    across = slot_of(z, 1 - x, c)
    beside = slot_of(z, x, 1 - c)

    def spread(s, act):
        if s == 0:
            pl.when(z < nz - 1)(lambda: act(send(0, me, right)))
            pl.when(z > 0)(lambda: act(send(1, me, left)))
            act(send(2, me, across))
            act(send(3, me, beside))
            return
        low, high = slot_of(z - s, x, c), slot_of(z + s, x, c)

        @pl.when(z - s >= 0)
        def _():
            if act is start:
                arrived(low)
            pl.when(z < nz - 1)(lambda: act(send(0, low, right)))
            act(send(2, low, across))
            act(send(3, low, beside))

        @pl.when(z + s < nz)
        def _():
            if act is start:
                arrived(high)
            pl.when(z > 0)(lambda: act(send(1, high, left)))
            act(send(2, high, across))
            act(send(3, high, beside))

    def hand_over(s, act):
        def one(slot):
            if act is start:
                arrived(slot)
            act(send(3, slot, beside))

        if s == 0:
            one(slot_of(z, 1 - x, c))
            return
        pl.when(z - s >= 0)(lambda: one(slot_of(z - s, 1 - x, c)))
        pl.when(z + s < nz)(lambda: one(slot_of(z + s, 1 - x, c)))

    def start(copy):
        copy.start()

    def sent(copy):
        copy.wait_send()

    spread(0, start)
    store(me).start()

    loads[2].wait()
    tq = min(512, hq)

    def q_tile(t, carry):
        cols = pl.ds(pl.multiple_of(t * tq, tq), tq)
        q_ref[:, cols] = jnp.dot(normed[...], wq[:, cols], preferred_element_type=F32).astype(BF16)
        return carry

    lax.fori_loop(0, hq // tq, q_tile, 0)
    q_store = pltpu.make_async_copy(q_ref, q_out, osem.at[0])
    q_store.start()
    spread(1, start)

    own[1].wait()
    for copy in dyc:
        copy.wait()
    loads[3].wait()

    def do_tile(t, carry):
        cols = pl.ds(pl.multiple_of(t * tq, tq), tq)
        acc = jnp.zeros((rows, tq), F32)
        for j in range(nh):
            acc = acc + lax.dot_general(
                dyall[j], wo[cols, j * share:(j + 1) * share], NT, preferred_element_type=F32)
        do_ref[:, cols] = acc.astype(BF16)
        return carry

    tiles = hq // tq
    gaps = nz - 2
    for s in range(2, nz):
        lax.fori_loop(tiles * (s - 2) // gaps, tiles * (s - 1) // gaps, do_tile, 0)
        if s == nz - 1:
            do_store = pltpu.make_async_copy(do_ref, do_out, osem.at[1])
            do_store.start()
        spread(s, start)
        hand_over(s - 2, start)

    product = jnp.zeros((rows, 1), F32)
    for j in range(nh):
        product = product + jnp.sum(
            xall[j].astype(F32) * dyall[j].astype(F32), axis=1, keepdims=True)
    stat_ref[:, 0:128] = jnp.broadcast_to(inv, (rows, 128))
    stat_ref[:, 128:256] = jnp.broadcast_to(product, (rows, 128))
    stat_ref[:, 256:384] = jnp.broadcast_to(total * inv * inv, (rows, 128))

    for s in range(nz - 2, nz):
        hand_over(s, start)
    for zz in range(nz):
        for xx in range(2):
            arrived(slot_of(zz, xx, 1 - c))
    for s in range(nz):
        spread(s, sent)
        hand_over(s, sent)
    for slot in range(4 * nz):
        store(slot).wait()
    q_store.wait()
    do_store.wait()


def front(nz, nh, order, lengths, x, dy, gain, wq, wk, wv, wo):
    rows, share = x.shape
    hq, width = wq.shape[1], wk.shape[1]
    n = 4 * nz
    dma = pltpu.SemaphoreType.DMA
    return pl.pallas_call(
        functools.partial(front_kernel, nz, nh),
        out_shape=(
            jax.ShapeDtypeStruct((rows, hq), BF16),
            jax.ShapeDtypeStruct((rows, hq), BF16),
            jax.ShapeDtypeStruct((n * rows, 2 * width), BF16),
            jax.ShapeDtypeStruct((rows, 384), F32),
            jax.ShapeDtypeStruct((rows, 2), jnp.int32),
            jax.ShapeDtypeStruct((2, n * rows), jnp.int32),
        ),
        in_specs=[SM, SM, VM, VM, VM, ANY, ANY, ANY, ANY],
        out_specs=(ANY, ANY, ANY, VM, VM, VM),
        scratch_shapes=[
            pltpu.VMEM((rows, hq), BF16), pltpu.VMEM((rows, hq), BF16),
            pltpu.VMEM((n * rows, 2 * width), BF16),
            pltpu.VMEM(wq.shape, BF16), pltpu.VMEM(wk.shape, BF16),
            pltpu.VMEM(wv.shape, BF16), pltpu.VMEM(wo.shape, BF16),
            pltpu.VMEM((nh, rows, share), BF16), pltpu.VMEM((nh, rows, share), BF16),
            pltpu.VMEM((rows, nh * share), BF16),
            dma((4,)), dma((2,)), dma((2,)), dma((n,)), dma((nh,)), dma((nh,)), dma((nh,)), dma((nh,)),
            dma((4, n)), dma((n,)),
        ],
        compiler_params=pltpu.CompilerParams(
            collective_id=0, has_side_effects=True, vmem_limit_bytes=VMEM_LIMIT),
        name="front",
    )(order, lengths, x, dy, gain, wq, wk, wv, wo)


def back_kernel(nz, nh, chunk, pq_ref, pk_ref, q_ref, do_ref, kv_hbm, x_ref, dy_ref, gain_ref,
                stat_ref, wq_ref, wk_ref, wv_ref, out_ref, sal_ref,
                kv_ref, wq, wk, wv, bias, ds_all, p_all, dq, dkv, hidden,
                core_in, x_out, x_in, low_out, low_in, high_out, high_in,
                grads, h_out, h_in, part_out, part_in,
                gsem, wsem, cs, cr, xs, xr, ls, lr, us, ur, hs, hr, ps, pr):
    me, z, x, c = coords()
    head = lax.axis_index("head")
    rows, share = x_ref.shape
    dim = nh * share
    hq = q_ref.shape[1]
    width = wk_ref.shape[1]
    kvh = width // HEAD_DIM
    per_group = hq // width
    scale = HEAD_DIM ** (-0.5)

    def kv_load(g, kind):
        at = pl.ds(pl.multiple_of(kind * width + g * HEAD_DIM, HEAD_DIM), HEAD_DIM)
        return pltpu.make_async_copy(kv_hbm.at[:, at], kv_ref.at[:, at], gsem.at[kind, g])

    for g in range(kvh):
        kv_load(g, 0).start()
        kv_load(g, 1).start()
    loads = [
        pltpu.make_async_copy(a, b, wsem.at[i])
        for i, (a, b) in enumerate(((wq_ref, wq), (wk_ref, wk), (wv_ref, wv)))
    ]
    for load in loads:
        load.start()
    enter(nz, nh)
    place, owner = pq_ref[:, 0:1], pq_ref[:, 1:2]
    allowed = (owner == pk_ref[1:2, :]) & (pk_ref[0:1, :] <= place)
    bias[...] = jnp.where(allowed, 0.0, -1e30)

    def lanes(start, size):
        return pl.ds(pl.multiple_of(start, HEAD_DIM), size)

    def part(g, slot):
        return (g, slice(None), pl.ds(pl.multiple_of(slot * rows, rows), rows), slice(None))

    def remote(src, dst, ss, rs, target):
        return pltpu.make_async_remote_copy(
            src_ref=src, dst_ref=dst, send_sem=ss, recv_sem=rs, device_id=target,
            device_id_type=MESH)

    beside = {"ctx": slot_of(z, x, 1 - c)}
    across = {"ctx": slot_of(z, 1 - x, c)}
    right = {"ctx": slot_of(z + 1, x, c)}
    left = {"ctx": slot_of(z - 1, x, c)}

    def core_copy(g, k, zz):
        xx = 1 - x if k == 0 else x
        return remote(dkv.at[part(g, slot_of(zz, xx, 1 - c))], core_in.at[g, k, zz],
                      cs.at[g, k, zz], cr.at[g, k, zz], beside)

    def x_copy(g, zz):
        return remote(x_out.at[g, zz], x_in.at[g, zz], xs.at[g, zz], xr.at[g, zz], across)

    def up_copy(g, zz):
        return remote(high_out.at[g, zz], high_in.at[g, zz], us.at[g, zz], ur.at[g, zz], right)

    def down_copy(g, zz):
        return remote(low_out.at[g, zz], low_in.at[g, zz], ls.at[g, zz], lr.at[g, zz], left)

    def target_of(i):
        if i == nz - 1:
            return z
        high = nz - 1 - i - jnp.where(i >= nz - 1 - z, 1, 0)
        low = i + jnp.where(i >= z, 1, 0)
        return jnp.where(z < nz // 2, high, low)

    def cross(g):
        for i in range(nz):
            zz = target_of(i)
            core_copy(g, 0, zz).wait_recv()
            x_out[g, zz] = (dkv[part(g, slot_of(zz, 1 - x, c))].astype(F32)
                            + core_in[g, 0, zz].astype(F32)).astype(BF16)
            x_copy(g, zz).start()

    def local_sum(g, zz):
        core_copy(g, 1, zz).wait_recv()
        x_copy(g, zz).wait_recv()
        return (dkv[part(g, slot_of(zz, x, c))].astype(F32) + core_in[g, 1, zz].astype(F32)
                + x_in[g, zz].astype(F32))

    def tick(g, tau):
        @pl.when(z <= tau)
        def _():
            zz = nz - 1 - tau + z
            high_out[g, zz] = local_sum(g, zz).astype(BF16)

            @pl.when(z > 0)
            def _():
                up_copy(g, zz).wait_recv()
                high_out[g, zz] = (high_out[g, zz].astype(F32)
                                   + high_in[g, zz].astype(F32)).astype(BF16)

            up_copy(g, zz).start()

        @pl.when(nz - 1 - z <= tau)
        def _():
            zz = tau - (nz - 1 - z)
            low_out[g, zz] = local_sum(g, zz).astype(BF16)

            @pl.when(z < nz - 1)
            def _():
                down_copy(g, zz).wait_recv()
                low_out[g, zz] = (low_out[g, zz].astype(F32)
                                  + low_in[g, zz].astype(F32)).astype(BF16)

            down_copy(g, zz).start()

    def settle(g):
        at = lanes(g * HEAD_DIM, HEAD_DIM)
        grads[:, :, at] = local_sum(g, z)

        @pl.when(z > 0)
        def _():
            up_copy(g, z).wait_recv()
            grads[:, :, at] = grads[:, :, at] + high_in[g, z].astype(F32)

        @pl.when(z < nz - 1)
        def _():
            down_copy(g, z).wait_recv()
            grads[:, :, at] = grads[:, :, at] + low_in[g, z].astype(F32)

    def attend(g, h):
        k = kv_ref[:, lanes(g * HEAD_DIM, HEAD_DIM)]
        v = kv_ref[:, lanes(width + g * HEAD_DIM, HEAD_DIM)]
        cols = lanes((g * per_group + h) * HEAD_DIM, HEAD_DIM)
        band = slice(h * rows, (h + 1) * rows)
        q, do = q_ref[:, cols], do_ref[:, cols]
        s = lax.dot_general(q, k, NT, preferred_element_type=F32) * scale + bias[...]
        e = jnp.exp(s - jnp.max(s, axis=1, keepdims=True))
        p = e * (1.0 / jnp.sum(e, axis=1, keepdims=True))
        half = p.astype(BF16)
        p_all[band, :] = half
        attended = jnp.dot(half, v, preferred_element_type=F32).astype(BF16)
        delta = jnp.sum(do.astype(F32) * attended.astype(F32), axis=1, keepdims=True)
        dp = lax.dot_general(do, v, NT, preferred_element_type=F32)
        ds = (p * (dp - delta) * scale).astype(BF16)
        ds_all[band, :] = ds
        dq[:, cols] = jnp.dot(ds, k, preferred_element_type=F32).astype(BF16)

    def group_grads(g):
        heads = [lanes((g * per_group + h) * HEAD_DIM, HEAD_DIM) for h in range(per_group)]
        qs = jnp.concatenate([q_ref[:, at] for at in heads], axis=0)
        dos = jnp.concatenate([do_ref[:, at] for at in heads], axis=0)
        dk = lax.dot_general(qs, ds_all[...], TN, preferred_element_type=F32)
        dkv[g, 0] = dk.astype(BF16).T
        dv = lax.dot_general(dos, p_all[...], TN, preferred_element_type=F32)
        dkv[g, 1] = dv.astype(BF16).T
        for kind in range(2):
            for i in range(nz):
                core_copy(g, kind, target_of(i)).start()

    tile = 512
    tiles = dim // tile

    def h_tile(t, carry):
        at = pl.ds(pl.multiple_of(t * tile, tile), tile)
        hidden[:, at] = lax.dot_general(dq[...], wq[at, :], NT, preferred_element_type=F32)
        return carry

    def step(t, carry):
        @pl.when(t < kvh)
        def _():
            kv_load(t, 0).wait()
            kv_load(t, 1).wait()
            for h in range(per_group // 2):
                attend(t, h)

        @pl.when(t == kvh)
        def _():
            loads[0].wait()

        @pl.when(t >= kvh)
        def _():
            e = t - kvh
            lax.fori_loop(tiles * e // (nz + 1), tiles * (e + 1) // (nz + 1), h_tile, 0)

        for stage in range(1, nz + 2):
            g = t - stage

            @pl.when((g >= 0) & (g < kvh))
            def _():
                if stage == 1:
                    cross(g)
                elif stage <= nz:
                    tick(g, stage - 2)
                else:
                    settle(g)

        @pl.when(t < kvh)
        def _():
            for h in range(per_group // 2, per_group):
                attend(t, h)
            group_grads(t)

        return carry

    lax.fori_loop(0, kvh + nz + 1, step, 0)
    loads[1].wait()
    loads[2].wait()

    def finish(start):
        at = pl.ds(pl.multiple_of(start, chunk), chunk)
        return (hidden[:, at]
                + lax.dot_general(grads[0].astype(BF16), wk[at, :], NT, preferred_element_type=F32)
                + lax.dot_general(grads[1].astype(BF16), wv[at, :], NT, preferred_element_type=F32))

    per = share // chunk

    def h_copy(p, k):
        return remote(h_out.at[p - 1, k], h_in.at[p - 1, k], hs.at[p - 1, k], hr.at[p - 1, k],
                      {"head": lax.rem(head + p, nh)})

    for p in range(1, nh):
        for k in range(per):
            h_out[p - 1, k] = finish(lax.rem(head + p, nh) * share + k * chunk).astype(BF16)
            h_copy(p, k).start()
    inv = stat_ref[:, 0:1]
    product = stat_ref[:, 128:129]
    squares = stat_ref[:, 256:257]
    for k in range(per):
        hidden[:, k * chunk:(k + 1) * chunk] = finish(head * share + k * chunk)
    inner = jnp.zeros((rows, 1), F32)
    for k in range(per):
        cols = slice(k * chunk, (k + 1) * chunk)
        grad = hidden[:, cols]
        for p in range(1, nh):
            h_copy(p, k).wait_recv()
            grad = grad + h_in[p - 1, k].astype(F32)
        scaled = grad * gain_ref[:, pl.ds(pl.multiple_of(head * share + k * chunk, chunk), chunk)]
        hidden[:, cols] = scaled
        inner = inner + jnp.sum(scaled * (x_ref[:, cols].astype(F32) * inv), axis=1, keepdims=True)
    part_out[...] = jnp.broadcast_to(inner, part_out.shape)

    def p_copy(p):
        return remote(part_out, part_in.at[p - 1], ps.at[p - 1], pr.at[p - 1],
                      {"head": lax.rem(head + p, nh)})

    for p in range(1, nh):
        p_copy(p).start()
    for p in range(1, nh):
        p_copy(p).wait_recv()
        inner = inner + part_in[p - 1][:, 0:1]
    saliency = product + inner - (inner / dim) * squares
    sal_ref[...] = jnp.broadcast_to(saliency, (rows, 128)).T[0:1, :]
    inner = inner / dim
    for k in range(per):
        cols = slice(k * chunk, (k + 1) * chunk)
        unit = x_ref[:, cols].astype(F32) * inv
        out_ref[:, cols] = (dy_ref[:, cols].astype(F32)
                            + (hidden[:, cols] - unit * inner) * inv).astype(BF16)

    def drain(g, carry):
        for zz in range(nz):
            core_copy(g, 0, zz).wait_send()
            core_copy(g, 1, zz).wait_send()
            x_copy(g, zz).wait_send()
            pl.when(z < zz)(lambda zz=zz: up_copy(g, zz).wait_send())
            pl.when(z > zz)(lambda zz=zz: down_copy(g, zz).wait_send())
        return carry

    lax.fori_loop(0, kvh, drain, 0)
    for p in range(1, nh):
        for k in range(per):
            h_copy(p, k).wait_send()
        p_copy(p).wait_send()


def back(nz, nh, pq, pk, q, do, kv, x, dy, gain, stat, wq, wk, wv):
    rows, share = x.shape
    width = wk.shape[1]
    kvh = width // HEAD_DIM
    length = kv.shape[0]
    wide = q.shape[1] // kvh
    dim = nh * share
    chunk = min(512, share)
    per = share // chunk
    piece = (kvh, nz, 2, rows, HEAD_DIM)
    dma = pltpu.SemaphoreType.DMA
    peers = max(1, nh - 1)
    hops = dma((kvh, nz))
    return pl.pallas_call(
        functools.partial(back_kernel, nz, nh, chunk),
        out_shape=(
            jax.ShapeDtypeStruct((rows, share), BF16),
            jax.ShapeDtypeStruct((1, rows), F32),
        ),
        in_specs=[VM] * 4 + [ANY] + [VM] * 4 + [ANY] * 3,
        out_specs=(VM, VM),
        scratch_shapes=[
            pltpu.VMEM(kv.shape, BF16),
            pltpu.VMEM(wq.shape, BF16), pltpu.VMEM(wk.shape, BF16), pltpu.VMEM(wv.shape, BF16),
            pltpu.VMEM((rows, length), F32),
            pltpu.VMEM((wide // HEAD_DIM * rows, length), BF16),
            pltpu.VMEM((wide // HEAD_DIM * rows, length), BF16),
            pltpu.VMEM(q.shape, BF16),
            pltpu.VMEM((kvh, 2, length, HEAD_DIM), BF16),
            pltpu.VMEM((rows, dim), F32),
            pltpu.VMEM((kvh, 2, nz, 2, rows, HEAD_DIM), BF16),
            pltpu.VMEM(piece, BF16), pltpu.VMEM(piece, BF16),
            pltpu.VMEM(piece, BF16), pltpu.VMEM(piece, BF16),
            pltpu.VMEM(piece, BF16), pltpu.VMEM(piece, BF16),
            pltpu.VMEM((2, rows, width), F32),
            pltpu.VMEM((peers, per, rows, chunk), BF16),
            pltpu.VMEM((peers, per, rows, chunk), BF16),
            pltpu.VMEM((rows, 128), F32), pltpu.VMEM((peers, rows, 128), F32),
            dma((2, kvh)), dma((3,)), dma((kvh, 2, nz)), dma((kvh, 2, nz)),
            hops, hops, hops, hops, hops, hops,
            dma((peers, per)), dma((peers, per)), dma((peers,)), dma((peers,)),
        ],
        compiler_params=pltpu.CompilerParams(
            collective_id=1, has_side_effects=True, vmem_limit_bytes=VMEM_LIMIT),
        name="back",
    )(pq, pk, q, do, kv, x, dy, gain, stat, wq, wk, wv)


def local(inputs, out_grad, norm_gain, w_query, w_key, w_value, w_out, record_lengths, block_order):
    rows, share = inputs.shape
    n = lax.axis_size("ctx")
    nh = lax.axis_size("head")
    nz = n // 4
    gain = norm_gain[None, :]
    q, do, kv, stat, pq, pk = front(
        nz, nh, block_order, record_lengths, inputs, out_grad, gain,
        w_query, w_key, w_value, w_out)
    input_grad, saliency = back(
        nz, nh, pq, pk, q, do, kv, inputs, out_grad, gain, stat, w_query, w_key, w_value)
    return (input_grad, saliency.reshape(rows))


def solution(mesh):
    placed = (
        P("ctx", "head"),
        P("ctx", "head"),
        P(),
        P(None, "head"),
        P(None, "head"),
        P(None, "head"),
        P("head", None),
        P(),
        P(),
    )
    return jax.shard_map(
        local, mesh=mesh, in_specs=placed, out_specs=(P("ctx", "head"), P("ctx")), check_vma=False
    )
```

profile of v0, /device:TPU:8, one launch (start us, length us, event | category | flops | bytes accessed | tf_op | source)
XLA Modules:
  0.0 114.6 jit_solution(9667849255081342897)
XLA Ops:
  0.6 45.0 %front.1 = (bf16[128,2048]{1,0:T(8,128)(2,1)}, bf16[128,2048]{1,0:T(8,128)(2,1)}, bf16[2048,1024]{1,0:T(8,128)(2,1)}, f32[128,384]{1,0:T(8,128)}, s32[128,2]{1,0:T(8,128)}, /*index=5*/s32[2,2048]{1,0:T(2,128)}) custom-call(s32[32]{0:T(128)} %order_ref.1, s32[8]{0:T(128)} %lengths_ref.1, bf16[128,2048]{1,0:T(8,128)(2,1)} %x_ref.3, bf16[128,2048]{1,0:T(8,128)(2,1)} %dy_ref.3, ...), custom_call_target="tpu_custom_call" | custom-call | tf_op jit(solution)/shard_map/front/pallas_call | solution.py:269
  45.6 65.8 %back.1 = (bf16[128,2048]{1,0:T(8,128)(2,1)}, f32[1,128]{1,0:T(1,128)}) custom-call(s32[128,2]{1,0:T(8,128)} %get-tuple-element.10.pq_ref, s32[2,2048]{1,0:T(2,128)} %get-tuple-element.11.pk_ref, bf16[128,2048]{1,0:T(8,128)(2,1)} %get-tuple-element.12.q_ref, bf16[128,2048]{1,0:T(8,128)(2,1)} %get-tuple-element.13.do_ref, ...), custom_call_target="tpu_custom_call" | custom-call | tf_op jit(solution)/shard_map/back/pallas_call | solution.py:582
  111.5 1.9 %copy.13 = bf16[128,2048]{1,0:T(8,128)(2,1)} copy(bf16[128,2048]{1,0:T(8,128)(2,1)} %get-tuple-element.20) | data formatting | bytes 1048576
  113.4 1.2 %copy.14 = f32[128]{0:T(128)} copy(f32[128]{0:T(128)} %bitcast.4) | data formatting | bytes 1024
where the time goes:
time: 115 us
  Pallas kernels  111 us (97%)
  local copies, waits for them, and re-layouts  3.07 us (3%)
    pallas_call x1, Pallas kernels, back(): pl.pallas_call(functools.partial(back_kernel, nz, nh, chunk), out_shape=(...  65.8 us
    pallas_call x1, Pallas kernels, front(): pl.pallas_call(functools.partial(front_kernel, nz, nh), out_shape=(jax.Sh...  45 us
    unnamed x2, local copies, waits for them, and re-layouts  3.07 us

commit v1 on v0

--- a/solution.py
+++ b/solution.py
@@ -9,6 +9,10 @@
 
 HEAD_DIM = 128
 BLOCK = 64
+SLAB = 4
+HALVES = 2
+LOG2E = 1.4426950408889634
+LN2 = 0.6931471805599453
 NT = (((1,), (1,)), ((), ()))
 TN = (((0,), (0,)), ((), ()))
 F32 = jnp.float32
@@ -614,12 +618,638 @@
     )(pq, pk, q, do, kv, x, dy, gain, stat, wq, wk, wv)
 
 
+def fused_kernel(nz, order_ref, lengths_ref, x_ref, dy_ref, gain_ref,
+                 wq_ref, wk_ref, wv_ref, wo_ref, out_ref, sal_ref,
+                 wq, wk, wv, wo, xall, dyall, xg, acc_kv, acc2, inv_ref, vx,
+                 kv_own, kvs, q_out, do_out, qs, dos, qt, dot_, bias, ee, acc_o, m_run, stat,
+                 dq_own, part, up_in, down_in, fin, dkvr,
+                 h_out, h_in, part_out, part_in,
+                 wsem, lsem, xs, xr, dys, dyr, ks, kr, zus, zds, zr, qsem, qr, dsem, dr,
+                 us, ur, ls, lr, gs, gr, fs, fr, hs, hr, ps, pr):
+    me, z, x, c = coords()
+    head = lax.axis_index("head")
+    rows, share = x_ref.shape
+    dim = 2 * share
+    width = wk_ref.shape[1]
+    slab = SLAB * rows
+    wide = wq_ref.shape[1] // SLAB
+    per_group = wide // HEAD_DIM
+    rc = rows // HALVES
+    block = SLAB * rc
+    kv = 2 * HEAD_DIM
+    scale = HEAD_DIM ** (-0.5)
+    j = x * 2 + c
+    gg = wo.at[:, 0:block]
+    dq_slab = wo.at[0:slab, block:block + wide]
+    peer = 1 - head
+    mine = pl.ds(pl.multiple_of(head * share, share), share)
+    theirs = pl.ds(pl.multiple_of(peer * share, share), share)
+
+    own = [
+        pltpu.make_async_copy(x_ref, xall.at[head], lsem.at[0]),
+        pltpu.make_async_copy(dy_ref, dyall.at[head], lsem.at[1]),
+    ]
+    own[0].start()
+    load_k = pltpu.make_async_copy(wk_ref, wk, wsem.at[0])
+    load_v = pltpu.make_async_copy(wv_ref, wv, wsem.at[1])
+    load_q = [pltpu.make_async_copy(wq_ref.at[at, :], wq.at[at, :], wsem.at[2 + i])
+              for i, at in enumerate((mine, theirs))]
+    load_o = [pltpu.make_async_copy(wo_ref.at[:, at], wo, wsem.at[4 + i])
+              for i, at in enumerate((mine, theirs))]
+    load_k.start()
+    load_v.start()
+    load_q[0].start()
+    own[1].start()
+    load_o[0].start()
+    load_q[1].start()
+
+    def member(p):
+        xx = x if p < 2 else 1 - x
+        cc = c if p % 2 == 0 else 1 - c
+        return xx, cc, xx * 2 + cc
+
+    barrier = pltpu.get_barrier_semaphore()
+
+    def greet(target):
+        pl.semaphore_signal(barrier, inc=1, device_id=target, device_id_type=MESH)
+
+    greet({"head": peer})
+    for p in range(1, SLAB):
+        greet({"ctx": slot_of(z, *member(p)[:2])})
+    pl.when(z > 0)(lambda: greet({"ctx": slot_of(z - 1, x, c)}))
+    pl.when(z < nz - 1)(lambda: greet({"ctx": slot_of(z + 1, x, c)}))
+
+    @pl.when((z > 0) & (z < nz - 1))
+    def _():
+        pl.semaphore_wait(barrier, SLAB + 2)
+
+    @pl.when((z == 0) | (z == nz - 1))
+    def _():
+        pl.semaphore_wait(barrier, SLAB + 1)
+
+    def remote(src, dst, ss, rs, target):
+        return pltpu.make_async_remote_copy(
+            src_ref=src, dst_ref=dst, send_sem=ss, recv_sem=rs, device_id=target,
+            device_id_type=MESH)
+
+    def to_member(p, src, dst, ss, rs):
+        xx, cc, _ = member(p)
+        return remote(src, dst, ss, rs, {"ctx": slot_of(z, xx, cc)})
+
+    right = {"ctx": slot_of(z + 1, x, c)}
+    left = {"ctx": slot_of(z - 1, x, c)}
+
+    def span(start, size):
+        return pl.ds(pl.multiple_of(start, size), size)
+
+    def x_copy(a):
+        at = slice(a * rc, (a + 1) * rc)
+        return remote(x_ref.at[at, :], xall.at[head, at, :], xs.at[a], xr.at[a], {"head": peer})
+
+    tile = wide
+    fd = min(1024, share)
+    feats = share // fd
+
+    def dy_copy(f):
+        at = slice(f * fd, (f + 1) * fd)
+        return remote(dy_ref.at[:, at], dyall.at[head, :, at], dys.at[f], dyr.at[f], {"head": peer})
+
+    for a in range(HALVES):
+        x_copy(a).start()
+    for f in range(feats):
+        dy_copy(f).start()
+
+    def make_bias():
+        vx[:, HEAD_DIM:kv] = jnp.ones((slab, HEAD_DIM), BF16)
+        place_q, owner_q = timeline_place(
+            lax.broadcasted_iota(jnp.int32, (slab, 1), 0) + z * slab, order_ref, lengths_ref)
+        lane = lax.broadcasted_iota(jnp.int32, (1, nz * slab), 1)
+        chunk_bits = rc.bit_length() - 1
+        row_in = lane & (rc - 1)
+        member_in = jnp.right_shift(lane, chunk_bits) & (SLAB - 1)
+        half_in = jnp.right_shift(lane, chunk_bits + 2) & (HALVES - 1)
+        slab_in = jnp.right_shift(lane, slab.bit_length() - 1)
+        place_k, owner_k = timeline_place(
+            slab_in * slab + member_in * rows + half_in * rc + row_in, order_ref, lengths_ref)
+        for zz in range(nz):
+            for a in range(HALVES):
+                at = slice(zz * slab + a * block, zz * slab + (a + 1) * block)
+                allowed = (owner_q == owner_k[:, at]) & (place_k[:, at] <= place_q)
+                bias[zz, :, a * block:(a + 1) * block] = jnp.where(allowed, 0.0, -1e30).astype(BF16)
+
+    def squares(v):
+        return jnp.sum(v * v, axis=1, keepdims=True)
+
+    def kv_own_half():
+        own[0].wait()
+        v = xall[head].astype(F32)
+        inv_ref[:, 2:3] = squares(v)
+        xg[head] = (v * gain_ref[:, mine]).astype(BF16)
+        load_k.wait()
+        acc_kv[0] = jnp.dot(xg[head], wk[mine, :], preferred_element_type=F32)
+        load_v.wait()
+        acc_kv[1] = jnp.dot(xg[head], wv[mine, :], preferred_element_type=F32)
+
+    def q_half(t, carry):
+        at = span(t * tile, tile)
+        acc2[0, :, at] = jnp.dot(xg[head], wq[mine, at], preferred_element_type=F32)
+        return carry
+
+    def do_half(t, carry):
+        at = span(t * tile, tile)
+        acc2[1, :, at] = lax.dot_general(dyall[head], wo[at, :], NT, preferred_element_type=F32)
+        return carry
+
+    def q_own():
+        load_q[0].wait()
+        lax.fori_loop(0, SLAB, q_half, 0)
+
+    def do_own(first, last):
+        if first == 0:
+            own[1].wait()
+            load_o[0].wait()
+        lax.fori_loop(first, last, do_half, 0)
+        if last == SLAB:
+            load_o[1].start()
+
+    def kv_copy(p, a):
+        jt = member(p)[2]
+        dst = kvs.at[z, a, span(j * rc, rc), :]
+        return to_member(p, kv_own.at[a, jt], dst, ks.at[a, p], kr.at[a, j])
+
+    def kv_arrived(p, a):
+        jt = member(p)[2]
+        to_member(p, kv_own.at[a, jt], kvs.at[z, a, span(jt * rc, rc), :],
+                  ks.at[a, p], kr.at[a, jt]).wait_recv()
+
+    def make_kv(a):
+        x_copy(a).wait_recv()
+        at = slice(a * rc, (a + 1) * rc)
+        v = xall[peer, at, :].astype(F32)
+        total = inv_ref[at, 2:3] + squares(v)
+        inv = 1.0 / jnp.sqrt(total / dim + 1e-05)
+        inv_ref[at, 0:1] = inv
+        inv_ref[at, 1:2] = total * inv * inv
+        xg[peer, at, :] = (v * gain_ref[:, theirs]).astype(BF16)
+        lhs = xg[peer, at, :]
+        for i, w in enumerate((wk, wv)):
+            got = (acc_kv[i, at, :] + jnp.dot(lhs, w[theirs, :], preferred_element_type=F32)) * inv
+            got = got.astype(BF16)
+            for jj in range(SLAB):
+                kv_own[a, jj, :, i * HEAD_DIM:(i + 1) * HEAD_DIM] = (
+                    got[:, jj * HEAD_DIM:(jj + 1) * HEAD_DIM])
+        for p in (2, 3, 1):
+            kv_copy(p, a).start()
+        kvs[z, a, span(j * rc, rc), :] = kv_own[a, j]
+
+    def piece(zz, a, s):
+        return kvs.at[zz, a, span(s * 2 * rc, 2 * rc), :]
+
+    def z_up(zz, a, s):
+        return remote(piece(zz, a, s), piece(zz, a, s), zus.at[zz, a, s], zr.at[zz, a, s], right)
+
+    def z_down(zz, a, s):
+        return remote(piece(zz, a, s), piece(zz, a, s), zds.at[zz, a, s], zr.at[zz, a, s], left)
+
+    def gather_own(a):
+        kv_arrived(1, a)
+        for s, peers in ((x, ()), (1 - x, (2, 3))):
+            for p in peers:
+                kv_arrived(p, a)
+            pl.when(z < nz - 1)(lambda s=s: z_up(z, a, s).start())
+            pl.when(z > 0)(lambda s=s: z_down(z, a, s).start())
+
+    def order(t):
+        near = jnp.where(z < nz // 2, z, nz - 1 - z)
+        d = (t + 1) // 2
+        o = jnp.where(t <= 2 * near, near + d if t % 2 else near - d, t)
+        return jnp.where(z < nz // 2, o, nz - 1 - o)
+
+    def take(t, a):
+        zz = order(t)
+        for s in range(2):
+            z_up(zz, a, s).wait_recv()
+            pl.when((zz < z) & (z < nz - 1))(lambda s=s: z_up(zz, a, s).start())
+            pl.when((zz > z) & (z > 0))(lambda s=s: z_down(zz, a, s).start())
+
+    def shared(p, src, dst, ss, rs):
+        jt = member(p)[2]
+        return to_member(p, src.at[jt], dst.at[span(j * rows, rows), :], ss.at[p], rs.at[j])
+
+    def shared_arrived(p, src, dst, ss, rs):
+        jt = member(p)[2]
+        to_member(p, src.at[jt], dst.at[span(jt * rows, rows), :], ss.at[p], rs.at[jt]).wait_recv()
+
+    def q_tile(p):
+        jt = member(p)[2]
+        at = span(jt * tile, tile)
+        got = acc2[0, :, at] + jnp.dot(
+            xg[peer], wq[theirs, at], preferred_element_type=F32)
+        q_out[jt] = (got * (inv_ref[:, 0:1] * (scale * LOG2E))).astype(BF16)
+        if p:
+            shared(p, q_out, qs, qsem, qr).start()
+        else:
+            qs[span(j * rows, rows), :] = q_out[jt]
+
+    def do_part(f, first=0, last=SLAB):
+        if f == 0 and first == 0:
+            load_o[1].wait()
+        if first == 0:
+            dy_copy(f).wait_recv()
+        at = slice(f * fd, (f + 1) * fd)
+        if f < feats - 1:
+            def body(t, carry):
+                cols = span(t * tile, tile)
+                acc2[1, :, cols] = acc2[1, :, cols] + lax.dot_general(
+                    dyall[peer, :, at], wo[cols, at], NT, preferred_element_type=F32)
+                return carry
+
+            lax.fori_loop(first, last, body, 0)
+            return
+        for p in (3, 2, 1, 0):
+            jt = member(p)[2]
+            cols = span(jt * tile, tile)
+            do_out[jt] = (acc2[1, :, cols] + lax.dot_general(
+                dyall[peer, :, at], wo[cols, at], NT, preferred_element_type=F32)).astype(BF16)
+            if p:
+                shared(p, do_out, dos, dsem, dr).start()
+            else:
+                dos[span(j * rows, rows), :] = do_out[jt]
+
+    lane_at = lax.broadcasted_iota(jnp.int32, (slab, HEAD_DIM), 1)
+
+    def forward(t, hook=None):
+        zz = order(t)
+        vx[:, 0:HEAD_DIM] = kvs[zz, :, :, HEAD_DIM:kv].reshape(slab, HEAD_DIM)
+        def one(hh):
+            cols = span(hh * HEAD_DIM, HEAD_DIM)
+            k = kvs[zz, :, :, 0:HEAD_DIM].reshape(slab, HEAD_DIM)
+            s = lax.dot_general(qs[:, cols], k, NT, preferred_element_type=F32)
+            s = s + bias[zz].astype(F32)
+            m = jnp.broadcast_to(jnp.max(s, axis=1, keepdims=True), (slab, HEAD_DIM))
+            if t:
+                old = m_run[hh]
+                m = jnp.maximum(m, old)
+            half = jnp.exp2(s - jnp.concatenate([m] * SLAB, axis=1)).astype(BF16)
+            ee[t, span(hh * slab, slab), :] = half
+            o = jnp.dot(half, vx[...], preferred_element_type=F32)
+            if t:
+                alpha = jnp.exp2(old - m)
+                o = o + acc_o[hh] * jnp.concatenate([alpha, alpha], axis=1)
+            stat[hh] = jnp.where(lane_at == t, m, stat[hh]) if t else m
+            m_run[hh] = m
+            acc_o[hh] = o
+
+        def pair(i, carry):
+            one(2 * i)
+            one(2 * i + 1)
+            if hook is not None:
+                pl.when(i == 0)(hook)
+            return carry
+
+        lax.fori_loop(0, per_group // 2, pair, 0)
+
+    def settle():
+        def one(hh, carry):
+            cols = span(hh * HEAD_DIM, HEAD_DIM)
+            do = dos[:, cols]
+            inv_l = 1.0 / acc_o[hh, :, HEAD_DIM:kv]
+            attended = (acc_o[hh, :, 0:HEAD_DIM] * inv_l).astype(BF16)
+            delta = jnp.sum(do.astype(F32) * attended.astype(F32), axis=1, keepdims=True)
+            stat[hh] = jnp.where(lane_at == HEAD_DIM - 1, delta, jnp.exp2(stat[hh] - m_run[hh]) * inv_l)
+            acc_o[hh, :, 0:HEAD_DIM] = jnp.zeros((slab, HEAD_DIM), F32)
+            dot_[:, span(hh * slab, slab)] = do.T
+            return carry
+
+        lax.fori_loop(0, per_group, one, 0)
+
+    def turn_q():
+        def one(hh, carry):
+            qt[:, span(hh * slab, slab)] = qs[:, span(hh * HEAD_DIM, HEAD_DIM)].T
+            return carry
+
+        lax.fori_loop(0, per_group, one, 0)
+
+    def backward(t, a):
+        zz = order(t)
+        half = slice(a * block, (a + 1) * block)
+
+        def one(hh):
+            k = kvs[zz, a, :, 0:HEAD_DIM]
+            v = kvs[zz, a, :, HEAD_DIM:kv]
+            cols = span(hh * HEAD_DIM, HEAD_DIM)
+            at = span(hh * slab, slab)
+            dp = lax.dot_general(dos[:, cols], v, NT, preferred_element_type=F32)
+            p = ee[t, at, half].astype(F32) * stat[hh, :, t:t + 1]
+            ee[t, at, half] = p.astype(BF16)
+            g = (p * (dp - stat[hh, :, 127:128])).astype(BF16)
+            gg[at, :] = g
+            acc_o[hh, :, 0:HEAD_DIM] = (acc_o[hh, :, 0:HEAD_DIM]
+                                        + jnp.dot(g, k, preferred_element_type=F32))
+
+        def pair(i, carry):
+            one(2 * i)
+            one(2 * i + 1)
+            return carry
+
+        lax.fori_loop(0, per_group // 2, pair, 0)
+        dk = jnp.dot(qt[...], gg[...], preferred_element_type=F32) * LN2
+        dv = jnp.dot(dot_[...], ee[t, :, half], preferred_element_type=F32)
+        part[zz, a, :, 0:HEAD_DIM] = dk.astype(BF16).T
+        part[zz, a, :, HEAD_DIM:kv] = dv.astype(BF16).T
+
+    def up_copy(zz, a):
+        return remote(part.at[zz, a], up_in.at[zz, a], us.at[zz, a], ur.at[zz, a], right)
+
+    def down_copy(zz, a):
+        return remote(part.at[zz, a], down_in.at[zz, a], ls.at[zz, a], lr.at[zz, a], left)
+
+    def send_part(t, a):
+        zz = order(t)
+        pl.when((zz > z) & (z == 0))(lambda: up_copy(zz, a).start())
+        pl.when((zz < z) & (z == nz - 1))(lambda: down_copy(zz, a).start())
+
+    def pass_part(t, a):
+        zz = order(t)
+
+        @pl.when((zz > z) & (z > 0))
+        def _():
+            up_copy(zz, a).wait_recv()
+            part[zz, a] = (part[zz, a].astype(F32) + up_in[zz, a].astype(F32)).astype(BF16)
+            up_copy(zz, a).start()
+
+        @pl.when((zz < z) & (z < nz - 1))
+        def _():
+            down_copy(zz, a).wait_recv()
+            part[zz, a] = (part[zz, a].astype(F32) + down_in[zz, a].astype(F32)).astype(BF16)
+            down_copy(zz, a).start()
+
+    def fin_copy(p, a):
+        jt = member(p)[2]
+        return to_member(p, fin.at[a, span(jt * rc, rc), :], dkvr.at[a, j], fs.at[a, p], fr.at[a, j])
+
+    def fin_arrived(p, a):
+        jt = member(p)[2]
+        to_member(p, fin.at[a, span(jt * rc, rc), :], dkvr.at[a, jt], fs.at[a, p],
+                  fr.at[a, jt]).wait_recv()
+
+    def finish_part(a):
+        fin[a] = part[z, a]
+
+        @pl.when(z > 0)
+        def _():
+            up_copy(z, a).wait_recv()
+            fin[a] = (fin[a].astype(F32) + up_in[z, a].astype(F32)).astype(BF16)
+
+        @pl.when(z < nz - 1)
+        def _():
+            down_copy(z, a).wait_recv()
+            fin[a] = (fin[a].astype(F32) + down_in[z, a].astype(F32)).astype(BF16)
+
+        for p in (3, 2, 1):
+            fin_copy(p, a).start()
+        dkvr[a, j] = fin[a, span(j * rc, rc), :]
+
+    def dq_copy(p):
+        jt = member(p)[2]
+        return to_member(p, wo.at[span(jt * rows, rows), block:block + wide], dq_own.at[:, span(j * tile, tile)],
+                         gs.at[p], gr.at[j])
+
+    def dq_arrived(p):
+        jt = member(p)[2]
+        to_member(p, wo.at[span(jt * rows, rows), block:block + wide], dq_own.at[:, span(jt * tile, tile)],
+                  gs.at[p], gr.at[jt]).wait_recv()
+
+    make_bias()
+    kv_own_half()
+    q_own()
+    make_kv(0)
+    do_own(0, 2)
+    gather_own(0)
+    do_own(2, SLAB)
+    make_kv(1)
+    load_q[1].wait()
+    q_tile(3)
+    q_tile(2)
+    q_tile(1)
+    q_tile(0)
+    take(1, 0)
+    gather_own(1)
+    do_part(0, 0, 2)
+    for t in range(2, min(3, nz)):
+        take(t, 0)
+    do_part(0, 2, SLAB)
+    take(1, 1)
+    for p in (1, 2, 3):
+        shared_arrived(p, q_out, qs, qsem, qr)
+
+    def far():
+        for t in range(3, nz):
+            take(t, 0)
+
+    forward(0, far)
+    for t in range(2, min(3, nz)):
+        take(t, 1)
+    for f in range(1, feats):
+        do_part(f)
+    forward(1)
+    for t in range(3, nz):
+        take(t, 1)
+    turn_q()
+    for t in range(2, nz):
+        forward(t)
+    for p in (1, 2, 3):
+        shared_arrived(p, do_out, dos, dsem, dr)
+    settle()
+    steps = [(nz - 1, a) for a in range(HALVES)]
+    steps += [(t, a) for a in range(HALVES) for t in range(nz - 2, 0, -1)]
+    steps += [(0, a) for a in range(HALVES)]
+    lag = 3
+    for i, (t, a) in enumerate(steps):
+        backward(t, a)
+        if t:
+            send_part(t, a)
+        if i >= lag and steps[i - lag][0]:
+            pass_part(*steps[i - lag])
+    for hh in range(per_group):
+        dq_slab[:, hh * HEAD_DIM:(hh + 1) * HEAD_DIM] = (acc_o[hh, :, 0:HEAD_DIM] * scale).astype(BF16)
+    for p in (3, 2, 1):
+        dq_copy(p).start()
+    dq_own[:, span(j * tile, tile)] = dq_slab[span(j * rows, rows), :]
+    for step in steps[len(steps) - lag:]:
+        if step[0]:
+            pass_part(*step)
+    product = jnp.zeros((rows, 1), F32)
+    for h in range(2):
+        product = product + jnp.sum(
+            xall[h].astype(F32) * dyall[h].astype(F32), axis=1, keepdims=True)
+    dq_arrived(1)
+    hidden = acc2
+    chunk = min(512, share)
+    per = share // chunk
+
+    def h_tile(half, xx, add):
+        heads_at = span(xx * 2 * tile, 2 * tile)
+
+        def body(k, carry):
+            at = span(half * share + k * chunk, chunk)
+            cols = span(k * chunk, chunk)
+            got = lax.dot_general(dq_own[:, heads_at], wq[at, heads_at], NT,
+                                  preferred_element_type=F32)
+            hidden[half, :, cols] = hidden[half, :, cols] + got if add else got
+            return carry
+
+        lax.fori_loop(0, per, body, 0)
+
+    h_tile(peer, x, False)
+    finish_part(0)
+    h_tile(head, x, False)
+    dq_arrived(3)
+    dq_arrived(2)
+    h_tile(peer, 1 - x, True)
+    finish_part(1)
+    h_tile(head, 1 - x, True)
+    for a in range(HALVES):
+        for p in (1, 2, 3):
+            fin_arrived(p, a)
+    grads = [
+        jnp.concatenate(
+            [jnp.concatenate([dkvr[a, jj, :, i * HEAD_DIM:(i + 1) * HEAD_DIM] for jj in range(SLAB)],
+                             axis=1) for a in range(HALVES)], axis=0)
+        for i in range(2)
+    ]
+
+    def finish(half, k):
+        at = span(half * share + k * chunk, chunk)
+        return (hidden[half, :, k * chunk:(k + 1) * chunk]
+                + lax.dot_general(grads[0], wk[at, :], NT, preferred_element_type=F32)
+                + lax.dot_general(grads[1], wv[at, :], NT, preferred_element_type=F32))
+
+    def h_copy(k):
+        return remote(h_out.at[k], h_in.at[k], hs.at[k], hr.at[k], {"head": peer})
+
+    inv = inv_ref[:, 0:1]
+    inner = jnp.zeros((rows, 1), F32)
+
+    def weighed(half, k, grad):
+        scaled = grad * gain_ref[:, span(half * share + k * chunk, chunk)]
+        unit = xall[half, :, k * chunk:(k + 1) * chunk].astype(F32) * inv
+        return jnp.sum(scaled * unit, axis=1, keepdims=True)
+
+    for k in range(per):
+        grad = finish(peer, k)
+        h_out[k] = grad.astype(BF16)
+        h_copy(k).start()
+        inner = inner + weighed(peer, k, grad)
+    for k in range(per):
+        grad = finish(head, k)
+        hidden[head, :, k * chunk:(k + 1) * chunk] = grad
+        inner = inner + weighed(head, k, grad)
+    part_out[...] = jnp.broadcast_to(inner, part_out.shape)
+    p_copy = remote(part_out, part_in, ps, pr, {"head": peer})
+    p_copy.start()
+    p_copy.wait_recv()
+    inner = inner + part_in[:, 0:1]
+    saliency = product + inner - (inner / dim) * inv_ref[:, 1:2]
+    sal_ref[...] = jnp.broadcast_to(saliency, (rows, 128)).T[0:1, :]
+    inner = inner / dim
+    for k in range(per):
+        cols = slice(k * chunk, (k + 1) * chunk)
+        unit = xall[head, :, cols].astype(F32) * inv
+        h_copy(k).wait_recv()
+        grad = hidden[head, :, cols] + h_in[k].astype(F32)
+        scaled = grad * gain_ref[:, span(head * share + k * chunk, chunk)]
+        out_ref[:, cols] = (dyall[head, :, cols].astype(F32)
+                            + (scaled - unit * inner) * inv).astype(BF16)
+
+    for a in range(HALVES):
+        x_copy(a).wait_send()
+        for p in (1, 2, 3):
+            kv_copy(p, a).wait_send()
+            fin_copy(p, a).wait_send()
+        for zz in range(nz):
+            pl.when(z < zz)(lambda zz=zz, a=a: up_copy(zz, a).wait_send())
+            pl.when(z > zz)(lambda zz=zz, a=a: down_copy(zz, a).wait_send())
+            for s in range(2):
+                pl.when((zz <= z) & (z < nz - 1))(lambda zz=zz, a=a, s=s: z_up(zz, a, s).wait_send())
+                pl.when((zz >= z) & (z > 0))(lambda zz=zz, a=a, s=s: z_down(zz, a, s).wait_send())
+    for f in range(feats):
+        dy_copy(f).wait_send()
+    for p in (1, 2, 3):
+        shared(p, q_out, qs, qsem, qr).wait_send()
+        shared(p, do_out, dos, dsem, dr).wait_send()
+        dq_copy(p).wait_send()
+    for k in range(per):
+        h_copy(k).wait_send()
+    p_copy.wait_send()
+
+
+def fused(nz, order, lengths, x, dy, gain, wq, wk, wv, wo):
+    rows, share = x.shape
+    dim = 2 * share
+    hq, width = wq.shape[1], wk.shape[1]
+    wide = hq // SLAB
+    heads = wide // HEAD_DIM
+    rc = rows // HALVES
+    slab = SLAB * rows
+    block = SLAB * rc
+    kv = 2 * HEAD_DIM
+    fd = min(1024, share)
+    chunk = min(512, share)
+    per = share // chunk
+    feats = share // fd
+    dma = pltpu.SemaphoreType.DMA
+    vm = pltpu.VMEM
+    return pl.pallas_call(
+        functools.partial(fused_kernel, nz),
+        out_shape=(
+            jax.ShapeDtypeStruct((rows, share), BF16),
+            jax.ShapeDtypeStruct((1, rows), F32),
+        ),
+        in_specs=[SM, SM, ANY, ANY, VM, ANY, ANY, ANY, ANY],
+        out_specs=(VM, VM),
+        scratch_shapes=[
+            vm(wq.shape, BF16), vm(wk.shape, BF16), vm(wv.shape, BF16), vm((hq, share), BF16),
+            vm((2, rows, share), BF16), vm((2, rows, share), BF16), vm((2, rows, share), BF16),
+            vm((2, rows, width), F32), vm((2, rows, share), F32), vm((rows, 128), F32),
+            vm((slab, kv), BF16),
+            vm((HALVES, SLAB, rc, kv), BF16), vm((nz, HALVES, block, kv), BF16),
+            vm((SLAB, rows, wide), BF16), vm((SLAB, rows, wide), BF16),
+            vm((slab, wide), BF16), vm((slab, wide), BF16),
+            vm((HEAD_DIM, heads * slab), BF16), vm((HEAD_DIM, heads * slab), BF16),
+            vm((nz, slab, slab), BF16),
+            vm((nz, heads * slab, slab), BF16),
+            vm((heads, slab, kv), F32), vm((heads, slab, HEAD_DIM), F32), vm((heads, slab, 128), F32),
+            vm((rows, hq), BF16),
+            vm((nz, HALVES, block, kv), BF16), vm((nz, HALVES, block, kv), BF16),
+            vm((nz, HALVES, block, kv), BF16),
+            vm((HALVES, block, kv), BF16), vm((HALVES, SLAB, rc, kv), BF16),
+            vm((per, rows, chunk), BF16), vm((per, rows, chunk), BF16),
+            vm((rows, 128), F32), vm((rows, 128), F32),
+            dma((6,)), dma((2,)), dma((HALVES,)), dma((HALVES,)), dma((feats,)), dma((feats,)),
+            dma((HALVES, SLAB)), dma((HALVES, SLAB)),
+            dma((nz, HALVES, 2)), dma((nz, HALVES, 2)), dma((nz, HALVES, 2)),
+            dma((SLAB,)), dma((SLAB,)), dma((SLAB,)), dma((SLAB,)),
+            dma((nz, HALVES)), dma((nz, HALVES)), dma((nz, HALVES)), dma((nz, HALVES)),
+            dma((SLAB,)), dma((SLAB,)), dma((HALVES, SLAB)), dma((HALVES, SLAB)),
+            dma((per,)), dma((per,)), dma(()), dma(()),
+        ],
+        compiler_params=pltpu.CompilerParams(
+            collective_id=2, has_side_effects=True, vmem_limit_bytes=VMEM_LIMIT),
+        name="fused",
+    )(order, lengths, x, dy, gain, wq, wk, wv, wo)
+
+
 def local(inputs, out_grad, norm_gain, w_query, w_key, w_value, w_out, record_lengths, block_order):
     rows, share = inputs.shape
     n = lax.axis_size("ctx")
     nh = lax.axis_size("head")
     nz = n // 4
     gain = norm_gain[None, :]
+    if nh == 2 and w_key.shape[1] == SLAB * HEAD_DIM:
+        input_grad, saliency = fused(
+            nz, block_order, record_lengths, inputs, out_grad, gain, w_query, w_key, w_value, w_out)
+        return (input_grad, saliency.reshape(rows))
     q, do, kv, stat, pq, pk = front(
         nz, nh, block_order, record_lengths, inputs, out_grad, gain,
         w_query, w_key, w_value, w_out)

time: 115 us -> 93.8 us (0.82)
  Pallas kernels: 111 us -> 89 us
    pallas_call x2 -> x1, Pallas kernels: 111 us -> 89 us  [fused(): pl.pallas_call(functools.partial(fused_kernel, nz), out_shape=(jax.ShapeD...]
where the time goes in v1:
time: 93.8 us; the launch traced here: 92.7 us
  Pallas kernels  89 us (95%)
  local copies, waits for them, and re-layouts  2.99 us (3%)
    pallas_call x1, Pallas kernels, fused(): pl.pallas_call(functools.partial(fused_kernel, nz), out_shape=(jax.ShapeD...  89 us
    unnamed x2, local copies, waits for them, and re-layouts  2.99 us

profile of v1, /device:TPU:8, one launch (start us, length us, event | category | flops | bytes accessed | tf_op | source)
XLA Modules:
  0.0 92.7 jit_solution(3986675583513200572)
XLA Ops:
  0.6 89.0 %fused.1 = (bf16[128,2048]{1,0:T(8,128)(2,1)}, f32[1,128]{1,0:T(1,128)}) custom-call(s32[32]{0:T(128)} %order_ref.1, s32[8]{0:T(128)} %lengths_ref.1, bf16[128,2048]{1,0:T(8,128)(2,1)} %x_ref.1, bf16[128,2048]{1,0:T(8,128)(2,1)} %dy_ref.1, f32[1,4096]{1,0:T(1,128)} %bitcast.2, bf16[4096,2048]{1,0:T(8,128)(2,1)} %wq_ref.1, bf16[4096,512]{1,0:T(8,128)(2,1)} %wk_ref.1, ...), custom_call_target="tpu_custom_call" | custom-call | tf_op jit(solution)/shard_map/fused/pallas_call | solution.py:1203
  89.7 1.9 %copy.13 = bf16[128,2048]{1,0:T(8,128)(2,1)} copy(bf16[128,2048]{1,0:T(8,128)(2,1)} %get-tuple-element.8) | data formatting | bytes 1048576
  91.6 1.1 %copy.14 = f32[128]{0:T(128)} copy(f32[128]{0:T(128)} %bitcast.3) | data formatting | bytes 1024

commit v2 on v1

--- a/solution.py
+++ b/solution.py
@@ -618,13 +618,13 @@
     )(pq, pk, q, do, kv, x, dy, gain, stat, wq, wk, wv)
 
 
-def fused_kernel(nz, order_ref, lengths_ref, x_ref, dy_ref, gain_ref,
+def fused_kernel(nz, order_hbm, lengths_hbm, x_ref, dy_ref, gain_hbm,
                  wq_ref, wk_ref, wv_ref, wo_ref, out_ref, sal_ref,
                  wq, wk, wv, wo, xall, dyall, xg, acc_kv, acc2, inv_ref, vx,
                  kv_own, kvs, q_out, do_out, qs, dos, qt, dot_, bias, ee, acc_o, m_run, stat,
                  dq_own, part, up_in, down_in, fin, dkvr,
-                 h_out, h_in, part_out, part_in,
-                 wsem, lsem, xs, xr, dys, dyr, ks, kr, zus, zds, zr, qsem, qr, dsem, dr,
+                 h_out, h_in, part_out, part_in, gain_ref, order_ref, lengths_ref,
+                 isem, wsem, lsem, xs, xr, dys, dyr, ks, kr, zus, zds, zr, qsem, qr, dsem, dr,
                  us, ur, ls, lr, gs, gr, fs, fr, hs, hr, ps, pr):
     me, z, x, c = coords()
     head = lax.axis_index("head")
@@ -649,6 +649,10 @@
         pltpu.make_async_copy(x_ref, xall.at[head], lsem.at[0]),
         pltpu.make_async_copy(dy_ref, dyall.at[head], lsem.at[1]),
     ]
+    small = [pltpu.make_async_copy(a, b, isem.at[i]) for i, (a, b) in enumerate(
+        ((order_hbm, order_ref), (lengths_hbm, lengths_ref), (gain_hbm, gain_ref)))]
+    for copy in small:
+        copy.start()
     own[0].start()
     load_k = pltpu.make_async_copy(wk_ref, wk, wsem.at[0])
     load_v = pltpu.make_async_copy(wv_ref, wv, wsem.at[1])
@@ -825,12 +829,27 @@
         o = jnp.where(t <= 2 * near, near + d if t % 2 else near - d, t)
         return jnp.where(z < nz // 2, o, nz - 1 - o)
 
+    def travels(zz):
+        return ((zz < z) & (z < nz - 1)) | ((zz > z) & (z > 0))
+
     def take(t, a):
         zz = order(t)
-        for s in range(2):
-            z_up(zz, a, s).wait_recv()
-            pl.when((zz < z) & (z < nz - 1))(lambda s=s: z_up(zz, a, s).start())
-            pl.when((zz > z) & (z > 0))(lambda s=s: z_down(zz, a, s).start())
+
+        @pl.when(travels(zz))
+        def _():
+            for s in range(2):
+                z_up(zz, a, s).wait_recv()
+                pl.when(zz < z)(lambda s=s: z_up(zz, a, s).start())
+                pl.when(zz > z)(lambda s=s: z_down(zz, a, s).start())
+
+    def keep(t):
+        zz = order(t)
+
+        @pl.when(jnp.logical_not(travels(zz)))
+        def _():
+            for a in range(HALVES):
+                for s in range(2):
+                    z_up(zz, a, s).wait_recv()
 
     def shared(p, src, dst, ss, rs):
         jt = member(p)[2]
@@ -1020,6 +1039,8 @@
         to_member(p, wo.at[span(jt * rows, rows), block:block + wide], dq_own.at[:, span(jt * tile, tile)],
                   gs.at[p], gr.at[jt]).wait_recv()
 
+    for copy in small:
+        copy.wait()
     make_bias()
     kv_own_half()
     q_own()
@@ -1052,11 +1073,13 @@
         take(t, 1)
     for f in range(1, feats):
         do_part(f)
+    keep(1)
     forward(1)
     for t in range(3, nz):
         take(t, 1)
     turn_q()
     for t in range(2, nz):
+        keep(t)
         forward(t)
     for p in (1, 2, 3):
         shared_arrived(p, do_out, dos, dsem, dr)
@@ -1103,12 +1126,10 @@
 
     h_tile(peer, x, False)
     finish_part(0)
-    h_tile(head, x, False)
+    finish_part(1)
     dq_arrived(3)
     dq_arrived(2)
     h_tile(peer, 1 - x, True)
-    finish_part(1)
-    h_tile(head, 1 - x, True)
     for a in range(HALVES):
         for p in (1, 2, 3):
             fin_arrived(p, a)
@@ -1141,15 +1162,17 @@
         h_out[k] = grad.astype(BF16)
         h_copy(k).start()
         inner = inner + weighed(peer, k, grad)
+    h_tile(head, x, False)
+    h_tile(head, 1 - x, True)
     for k in range(per):
         grad = finish(head, k)
         hidden[head, :, k * chunk:(k + 1) * chunk] = grad
         inner = inner + weighed(head, k, grad)
-    part_out[...] = jnp.broadcast_to(inner, part_out.shape)
+    part_out[...] = jnp.broadcast_to(inner, (rows, 128)).T[0:8, :]
     p_copy = remote(part_out, part_in, ps, pr, {"head": peer})
     p_copy.start()
     p_copy.wait_recv()
-    inner = inner + part_in[:, 0:1]
+    inner = inner + jnp.broadcast_to(part_in[0:1, :], (128, rows)).T[:, 0:1]
     saliency = product + inner - (inner / dim) * inv_ref[:, 1:2]
     sal_ref[...] = jnp.broadcast_to(saliency, (rows, 128)).T[0:1, :]
     inner = inner / dim
@@ -1206,7 +1229,7 @@
             jax.ShapeDtypeStruct((rows, share), BF16),
             jax.ShapeDtypeStruct((1, rows), F32),
         ),
-        in_specs=[SM, SM, ANY, ANY, VM, ANY, ANY, ANY, ANY],
+        in_specs=[ANY] * 9,
         out_specs=(VM, VM),
         scratch_shapes=[
             vm(wq.shape, BF16), vm(wk.shape, BF16), vm(wv.shape, BF16), vm((hq, share), BF16),
@@ -1225,8 +1248,9 @@
             vm((nz, HALVES, block, kv), BF16),
             vm((HALVES, block, kv), BF16), vm((HALVES, SLAB, rc, kv), BF16),
             vm((per, rows, chunk), BF16), vm((per, rows, chunk), BF16),
-            vm((rows, 128), F32), vm((rows, 128), F32),
-            dma((6,)), dma((2,)), dma((HALVES,)), dma((HALVES,)), dma((feats,)), dma((feats,)),
+            vm((8, rows), F32), vm((8, rows), F32),
+            vm((1, dim), F32), pltpu.SMEM(order.shape, jnp.int32), pltpu.SMEM(lengths.shape, jnp.int32),
+            dma((3,)), dma((6,)), dma((2,)), dma((HALVES,)), dma((HALVES,)), dma((feats,)), dma((feats,)),
             dma((HALVES, SLAB)), dma((HALVES, SLAB)),
             dma((nz, HALVES, 2)), dma((nz, HALVES, 2)), dma((nz, HALVES, 2)),
             dma((SLAB,)), dma((SLAB,)), dma((SLAB,)), dma((SLAB,)),

time: 93.8 us -> 89.7 us (0.956); the launches traced: 92.7 us -> 89.5 us
  Pallas kernels: 89 us -> 85.9 us
    pallas_call x1, Pallas kernels: 89 us -> 85.9 us  [fused(): pl.pallas_call(functools.partial(fused_kernel, nz), out_shape=(jax.ShapeD...]
where the time goes in v2:
time: 89.7 us; the launch traced here: 89.5 us
  Pallas kernels  85.9 us (96%)
  local copies, waits for them, and re-layouts  2.99 us (3%)
    pallas_call x1, Pallas kernels, fused(): pl.pallas_call(functools.partial(fused_kernel, nz), out_shape=(jax.ShapeD...  85.9 us
    unnamed x2, local copies, waits for them, and re-layouts  2.99 us

profile of v2, /device:TPU:8, one launch (start us, length us, event | category | flops | bytes accessed | tf_op | source)
XLA Modules:
  0.0 89.5 jit_solution(4997868757637866420)
XLA Ops:
  0.6 85.9 %fused.1 = (bf16[128,2048]{1,0:T(8,128)(2,1)}, f32[1,128]{1,0:T(1,128)}) custom-call(s32[32]{0:T(128)} %order_hbm.1, s32[8]{0:T(128)} %lengths_hbm.1, bf16[128,2048]{1,0:T(8,128)(2,1)} %x_ref.1, bf16[128,2048]{1,0:T(8,128)(2,1)} %dy_ref.1, f32[1,4096]{1,0:T(1,128)} %bitcast.2, bf16[4096,2048]{1,0:T(8,128)(2,1)} %wq_ref.1, bf16[4096,512]{1,0:T(8,128)(2,1)} %wk_ref.1, ...), custom_call_target="tpu_custom_call" | custom-call | tf_op jit(solution)/shard_map/fused/pallas_call | solution.py:1226
  86.5 1.9 %copy.13 = bf16[128,2048]{1,0:T(8,128)(2,1)} copy(bf16[128,2048]{1,0:T(8,128)(2,1)} %get-tuple-element.8) | data formatting | bytes 1048576
  88.4 1.1 %copy.14 = f32[128]{0:T(128)} copy(f32[128]{0:T(128)} %bitcast.3) | data formatting | bytes 1024

commit v3 on v2

--- a/solution.py
+++ b/solution.py
@@ -21,7 +21,7 @@
 VM = pl.BlockSpec(memory_space=pltpu.VMEM)
 ANY = pl.BlockSpec(memory_space=pl.ANY)
 SM = pl.BlockSpec(memory_space=pltpu.SMEM)
-VMEM_LIMIT = 64 * 1024 * 1024 - 128 * 1024
+VMEM_LIMIT = 67043328
 
 
 def timeline_place(stored, order_ref, lengths_ref):
@@ -622,8 +622,8 @@
                  wq_ref, wk_ref, wv_ref, wo_ref, out_ref, sal_ref,
                  wq, wk, wv, wo, xall, dyall, xg, acc_kv, acc2, inv_ref, vx,
                  kv_own, kvs, q_out, do_out, qs, dos, qt, dot_, bias, ee, acc_o, m_run, stat,
-                 dq_own, part, up_in, down_in, fin, dkvr,
-                 h_out, h_in, part_out, part_in, gain_ref, order_ref, lengths_ref,
+                 dq_own, part, up_in, down_in, dkvr,
+                 h_in, part_out, part_in, gain_ref, order_ref, lengths_ref,
                  isem, wsem, lsem, xs, xr, dys, dyr, ks, kr, zus, zds, zr, qsem, qr, dsem, dr,
                  us, ur, ls, lr, gs, gr, fs, fr, hs, hr, ps, pr):
     me, z, x, c = coords()
@@ -662,10 +662,7 @@
               for i, at in enumerate((mine, theirs))]
     load_k.start()
     load_v.start()
-    load_q[0].start()
     own[1].start()
-    load_o[0].start()
-    load_q[1].start()
 
     def member(p):
         xx = x if p < 2 else 1 - x
@@ -708,7 +705,7 @@
 
     def x_copy(a):
         at = slice(a * rc, (a + 1) * rc)
-        return remote(x_ref.at[at, :], xall.at[head, at, :], xs.at[a], xr.at[a], {"head": peer})
+        return remote(xall.at[head, at, :], xall.at[head, at, :], xs.at[a], xr.at[a], {"head": peer})
 
     tile = wide
     fd = min(1024, share)
@@ -716,12 +713,19 @@
 
     def dy_copy(f):
         at = slice(f * fd, (f + 1) * fd)
-        return remote(dy_ref.at[:, at], dyall.at[head, :, at], dys.at[f], dyr.at[f], {"head": peer})
-
+        return remote(dyall.at[head, :, at], dyall.at[head, :, at], dys.at[f], dyr.at[f], {"head": peer})
+
+    own[0].wait()
     for a in range(HALVES):
         x_copy(a).start()
+    own[1].wait()
     for f in range(feats):
         dy_copy(f).start()
+    for copy in small:
+        copy.wait()
+    load_q[0].start()
+    load_o[0].start()
+    load_q[1].start()
 
     def make_bias():
         vx[:, HEAD_DIM:kv] = jnp.ones((slab, HEAD_DIM), BF16)
@@ -745,7 +749,6 @@
         return jnp.sum(v * v, axis=1, keepdims=True)
 
     def kv_own_half():
-        own[0].wait()
         v = xall[head].astype(F32)
         inv_ref[:, 2:3] = squares(v)
         xg[head] = (v * gain_ref[:, mine]).astype(BF16)
@@ -770,7 +773,6 @@
 
     def do_own(first, last):
         if first == 0:
-            own[1].wait()
             load_o[0].wait()
         lax.fori_loop(first, last, do_half, 0)
         if last == SLAB:
@@ -1005,29 +1007,31 @@
 
     def fin_copy(p, a):
         jt = member(p)[2]
-        return to_member(p, fin.at[a, span(jt * rc, rc), :], dkvr.at[a, j], fs.at[a, p], fr.at[a, j])
+        return to_member(p, kv_own.at[a, jt], dkvr.at[a, j], fs.at[a, p], fr.at[a, j])
 
     def fin_arrived(p, a):
         jt = member(p)[2]
-        to_member(p, fin.at[a, span(jt * rc, rc), :], dkvr.at[a, jt], fs.at[a, p],
+        to_member(p, kv_own.at[a, jt], dkvr.at[a, jt], fs.at[a, p],
                   fr.at[a, jt]).wait_recv()
 
     def finish_part(a):
-        fin[a] = part[z, a]
+        kv_own[a] = part[z, a].reshape(SLAB, rc, kv)
 
         @pl.when(z > 0)
         def _():
             up_copy(z, a).wait_recv()
-            fin[a] = (fin[a].astype(F32) + up_in[z, a].astype(F32)).astype(BF16)
+            got = up_in[z, a].reshape(SLAB, rc, kv)
+            kv_own[a] = (kv_own[a].astype(F32) + got.astype(F32)).astype(BF16)
 
         @pl.when(z < nz - 1)
         def _():
             down_copy(z, a).wait_recv()
-            fin[a] = (fin[a].astype(F32) + down_in[z, a].astype(F32)).astype(BF16)
+            got = down_in[z, a].reshape(SLAB, rc, kv)
+            kv_own[a] = (kv_own[a].astype(F32) + got.astype(F32)).astype(BF16)
 
         for p in (3, 2, 1):
             fin_copy(p, a).start()
-        dkvr[a, j] = fin[a, span(j * rc, rc), :]
+        dkvr[a, j] = kv_own[a, j]
 
     def dq_copy(p):
         jt = member(p)[2]
@@ -1039,8 +1043,6 @@
         to_member(p, wo.at[span(jt * rows, rows), block:block + wide], dq_own.at[:, span(jt * tile, tile)],
                   gs.at[p], gr.at[jt]).wait_recv()
 
-    for copy in small:
-        copy.wait()
     make_bias()
     kv_own_half()
     q_own()
@@ -1065,18 +1067,20 @@
         shared_arrived(p, q_out, qs, qsem, qr)
 
     def far():
+        for t in range(2, min(3, nz)):
+            take(t, 1)
         for t in range(3, nz):
             take(t, 0)
 
+    def last():
+        for t in range(3, nz):
+            take(t, 1)
+
     forward(0, far)
-    for t in range(2, min(3, nz)):
-        take(t, 1)
     for f in range(1, feats):
         do_part(f)
     keep(1)
-    forward(1)
-    for t in range(3, nz):
-        take(t, 1)
+    forward(1, last)
     turn_q()
     for t in range(2, nz):
         keep(t)
@@ -1102,17 +1106,22 @@
     for step in steps[len(steps) - lag:]:
         if step[0]:
             pass_part(*step)
+    for p in (1, 2, 3):
+        shared(p, q_out, qs, qsem, qr).wait_send()
+        for a in range(HALVES):
+            kv_copy(p, a).wait_send()
     product = jnp.zeros((rows, 1), F32)
     for h in range(2):
         product = product + jnp.sum(
             xall[h].astype(F32) * dyall[h].astype(F32), axis=1, keepdims=True)
     dq_arrived(1)
     hidden = acc2
+    h_out = q_out
     chunk = min(512, share)
     per = share // chunk
 
-    def h_tile(half, xx, add):
-        heads_at = span(xx * 2 * tile, 2 * tile)
+    def h_tile(half, start, size, add):
+        heads_at = pl.ds(pl.multiple_of(start * tile, tile), size * tile)
 
         def body(k, carry):
             at = span(half * share + k * chunk, chunk)
@@ -1124,12 +1133,13 @@
 
         lax.fori_loop(0, per, body, 0)
 
-    h_tile(peer, x, False)
+    h_tile(peer, 2 * x, 2, False)
     finish_part(0)
     finish_part(1)
     dq_arrived(3)
+    h_tile(peer, member(3)[2], 1, True)
     dq_arrived(2)
-    h_tile(peer, 1 - x, True)
+    h_tile(peer, member(2)[2], 1, True)
     for a in range(HALVES):
         for p in (1, 2, 3):
             fin_arrived(p, a)
@@ -1162,8 +1172,8 @@
         h_out[k] = grad.astype(BF16)
         h_copy(k).start()
         inner = inner + weighed(peer, k, grad)
-    h_tile(head, x, False)
-    h_tile(head, 1 - x, True)
+    h_tile(head, 2 * x, 2, False)
+    h_tile(head, 2 * (1 - x), 2, True)
     for k in range(per):
         grad = finish(head, k)
         hidden[head, :, k * chunk:(k + 1) * chunk] = grad
@@ -1188,7 +1198,6 @@
     for a in range(HALVES):
         x_copy(a).wait_send()
         for p in (1, 2, 3):
-            kv_copy(p, a).wait_send()
             fin_copy(p, a).wait_send()
         for zz in range(nz):
             pl.when(z < zz)(lambda zz=zz, a=a: up_copy(zz, a).wait_send())
@@ -1199,7 +1208,6 @@
     for f in range(feats):
         dy_copy(f).wait_send()
     for p in (1, 2, 3):
-        shared(p, q_out, qs, qsem, qr).wait_send()
         shared(p, do_out, dos, dsem, dr).wait_send()
         dq_copy(p).wait_send()
     for k in range(per):
@@ -1246,8 +1254,8 @@
             vm((rows, hq), BF16),
             vm((nz, HALVES, block, kv), BF16), vm((nz, HALVES, block, kv), BF16),
             vm((nz, HALVES, block, kv), BF16),
-            vm((HALVES, block, kv), BF16), vm((HALVES, SLAB, rc, kv), BF16),
-            vm((per, rows, chunk), BF16), vm((per, rows, chunk), BF16),
+            vm((HALVES, SLAB, rc, kv), BF16),
+            vm((per, rows, chunk), BF16),
             vm((8, rows), F32), vm((8, rows), F32),
             vm((1, dim), F32), pltpu.SMEM(order.shape, jnp.int32), pltpu.SMEM(lengths.shape, jnp.int32),
             dma((3,)), dma((6,)), dma((2,)), dma((HALVES,)), dma((HALVES,)), dma((feats,)), dma((feats,)),
@@ -1270,7 +1278,7 @@
     nh = lax.axis_size("head")
     nz = n // 4
     gain = norm_gain[None, :]
-    if nh == 2 and w_key.shape[1] == SLAB * HEAD_DIM:
+    if nh == 2 and w_key.shape[1] == SLAB * HEAD_DIM and inputs.shape[1] == w_query.shape[1]:
         input_grad, saliency = fused(
             nz, block_order, record_lengths, inputs, out_grad, gain, w_query, w_key, w_value, w_out)
         return (input_grad, saliency.reshape(rows))

time: 89.7 us -> 85.5 us (0.953)
  Pallas kernels: 85.9 us -> 81.7 us
    pallas_call x1, Pallas kernels: 85.9 us -> 81.7 us  [fused(): pl.pallas_call(functools.partial(fused_kernel, nz), out_shape=(jax.ShapeD...]
where the time goes in v3:
time: 85.5 us; the launch traced here: 85.3 us
  Pallas kernels  81.7 us (96%)
  local copies, waits for them, and re-layouts  2.99 us (3%)
    pallas_call x1, Pallas kernels, fused(): pl.pallas_call(functools.partial(fused_kernel, nz), out_shape=(jax.ShapeD...  81.7 us
    unnamed x2, local copies, waits for them, and re-layouts  2.99 us

profile of v3, /device:TPU:8, one launch (start us, length us, event | category | flops | bytes accessed | tf_op | source)
XLA Modules:
  0.0 85.3 jit_solution(985939058112412760)
XLA Ops:
  0.6 81.7 %fused.1 = (bf16[128,2048]{1,0:T(8,128)(2,1)}, f32[1,128]{1,0:T(1,128)}) custom-call(s32[32]{0:T(128)} %order_hbm.1, s32[8]{0:T(128)} %lengths_hbm.1, bf16[128,2048]{1,0:T(8,128)(2,1)} %x_ref.1, bf16[128,2048]{1,0:T(8,128)(2,1)} %dy_ref.1, f32[1,4096]{1,0:T(1,128)} %bitcast.2, bf16[4096,2048]{1,0:T(8,128)(2,1)} %wq_ref.1, bf16[4096,512]{1,0:T(8,128)(2,1)} %wk_ref.1, ...), custom_call_target="tpu_custom_call" | custom-call | tf_op jit(solution)/shard_map/fused/pallas_call | solution.py:1234
  82.3 1.9 %copy.13 = bf16[128,2048]{1,0:T(8,128)(2,1)} copy(bf16[128,2048]{1,0:T(8,128)(2,1)} %get-tuple-element.8) | data formatting | bytes 1048576
  84.2 1.1 %copy.14 = f32[128]{0:T(128)} copy(f32[128]{0:T(128)} %bitcast.3) | data formatting | bytes 1024

commit v4 on v3

--- a/solution.py
+++ b/solution.py
@@ -1062,13 +1062,12 @@
     for t in range(2, min(3, nz)):
         take(t, 0)
     do_part(0, 2, SLAB)
-    take(1, 1)
+    for t in range(1, min(3, nz)):
+        take(t, 1)
     for p in (1, 2, 3):
         shared_arrived(p, q_out, qs, qsem, qr)
 
     def far():
-        for t in range(2, min(3, nz)):
-            take(t, 1)
         for t in range(3, nz):
             take(t, 0)
 
@@ -1079,8 +1078,9 @@
     forward(0, far)
     for f in range(1, feats):
         do_part(f)
+    last()
     keep(1)
-    forward(1, last)
+    forward(1)
     turn_q()
     for t in range(2, nz):
         keep(t)

time: 85.5 us -> 85.2 us (level)
  no operation moved by 1% of the time
where the time goes in v4:
time: 85.2 us; the launch traced here: 85.1 us
  Pallas kernels  81.4 us (96%)
  local copies, waits for them, and re-layouts  2.99 us (4%)
    pallas_call x1, Pallas kernels, fused(): pl.pallas_call(functools.partial(fused_kernel, nz), out_shape=(jax.ShapeD...  81.4 us
    unnamed x2, local copies, waits for them, and re-layouts  2.99 us

profile of v4, /device:TPU:8, one launch (start us, length us, event | category | flops | bytes accessed | tf_op | source)
XLA Modules:
  0.0 85.1 jit_solution(5965715260579473433)
XLA Ops:
  0.6 81.4 %fused.1 = (bf16[128,2048]{1,0:T(8,128)(2,1)}, f32[1,128]{1,0:T(1,128)}) custom-call(s32[32]{0:T(128)} %order_hbm.1, s32[8]{0:T(128)} %lengths_hbm.1, bf16[128,2048]{1,0:T(8,128)(2,1)} %x_ref.1, bf16[128,2048]{1,0:T(8,128)(2,1)} %dy_ref.1, f32[1,4096]{1,0:T(1,128)} %bitcast.2, bf16[4096,2048]{1,0:T(8,128)(2,1)} %wq_ref.1, bf16[4096,512]{1,0:T(8,128)(2,1)} %wk_ref.1, ...), custom_call_target="tpu_custom_call" | custom-call | tf_op jit(solution)/shard_map/fused/pallas_call | solution.py:1234
  82.1 1.9 %copy.13 = bf16[128,2048]{1,0:T(8,128)(2,1)} copy(bf16[128,2048]{1,0:T(8,128)(2,1)} %get-tuple-element.8) | data formatting | bytes 1048576
  84.0 1.1 %copy.14 = f32[128]{0:T(128)} copy(f32[128]{0:T(128)} %bitcast.3) | data formatting | bytes 1024
